TPU v7x, 256 devices: a whole 4x4x8 slice. The times are simulated.
256 devices in a mesh: seq: 32 (over z, y), mp: 4 (over x), req: 2 (over core).
Axes of the slice: x: 4, y: 4, z: 8, core: 2. Of those that a mesh axis runs over, the one named last changes fastest.
Arguments:
- hidden: bfloat16 [2, 8192, 3072], P('req', 'seq', 'mp'), may hold values from -6 to 6
- norm_gain: bfloat16 [3072], replicated, may hold values from 0.5 to 1.5
- w_query: bfloat16 [3072, 1024], P(None, 'mp'), may hold values from -0.109375 to 0.109375
- w_keyval: bfloat16 [3072, 512], P(None, 'mp'), may hold values from -0.109375 to 0.109375
- w_attn_out: bfloat16 [1024, 3072], P('mp'), may hold values from -1.5 to 1.5
- w_inner: bfloat16 [3072, 2, 1536], P(None, None, 'mp'), may hold values from -0.109375 to 0.109375
- w_bc: bfloat16 [3072, 512], P(None, 'mp'), may hold values from -0.109375 to 0.109375
- w_dt: bfloat16 [3072, 12], P(None, 'mp'), may hold values from -0.109375 to 0.109375
- dt_bias: float32 [12], P('mp'), may hold values from -4 to 0
- a_log: float32 [12], P('mp'), may hold values from -12 to 0
- d_skip: float32 [12], P('mp'), may hold values from 0.1 to 10
- conv_x: bfloat16 [4, 1536], P(None, 'mp'), may hold values from -3 to 3
- conv_bc: bfloat16 [4, 512], replicated, may hold values from -3 to 3
- mamba_gain: bfloat16 [1536], P('mp'), may hold values from 0.5 to 1.5
- w_mamba_out: bfloat16 [1536, 3072], P('mp'), may hold values from -0.15625 to 0.15625
- cache: bfloat16 [2, 8192, 512], P('req', 'seq', 'mp'), may hold values from -70 to 70, as said below
- cache_len: int32 [2], P('req'), may hold values from 256 to 8192
- tail_x: bfloat16 [2, 3, 1536], P('req', None, 'mp'), may hold values from -6 to 6
- tail_bc: bfloat16 [2, 3, 512], P('req'), may hold values from -6 to 6
- ssm_init: float32 [2, 12, 128, 256], P('req', 'mp'), may hold values from -6 to 6
Outputs:
- layer_out: bfloat16 [2, 8192, 3072], P('req', 'seq', 'mp')
- new_keyval: bfloat16 [2, 8192, 512], P('req', 'seq', 'mp')
- block_states: float32 [2, 32, 12, 128, 256], P('req', 'seq', 'mp')
Inputs may be any that keep to these rules, and one draw needn't show every extreme that they name: Rows of the cache at or past cache_len are unused.
All inputs are finite; a program needn't handle non-finite values.
Results may differ from a plain program's by a relative error of at most 0.0097.
Values may be sent and summed in bfloat16 or wider, within the bound.
A program may use at most 192 MiB of HBM per device.

v0:
```python
import jax
import jax.numpy as jnp
from jax import lax
from jax.sharding import PartitionSpec as P

HD = 128
QH = 8
KVH = 2
NS = 256
CONV = 4
epsilon = 1e-05
rope_base = 100000000000.0
negative = -1e30


def shifted(block, axis, distance):
    devices = range(lax.axis_size(axis))
    route = [(i - distance, i) for i in devices if i - distance in devices]
    return lax.ppermute(block, axis, route)


def prefix(part, axis, combine, identity):
    place = lax.axis_index(axis)
    gathered = jax.tree.map(lambda a: lax.all_gather(a, axis), part)
    state = jax.tree.map(lambda a, e: jnp.zeros_like(a) + jnp.asarray(e, a.dtype), part, identity)

    def one(turn, state):
        return combine(
            state, jax.tree.map(lambda a: lax.dynamic_index_in_dim(a, turn, 0, False), gathered)
        )

    return lax.fori_loop(0, place, one, state)


def rotate(values, positions):
    half = HD // 2
    freqs = rope_base ** (-jnp.arange(half, dtype=jnp.float32) * 2.0 / HD)
    angles = positions.astype(jnp.float32)[:, None] * freqs[None, :]
    cosine = jnp.cos(angles)[:, None, :]
    sine = jnp.sin(angles)[:, None, :]
    first = values[..., :half]
    second = values[..., half:]
    return jnp.concatenate(
        [first * cosine - second * sine, second * cosine + first * sine], axis=-1
    )


def rms_scale(values):
    mean_sq = jnp.mean(values * values, axis=-1, keepdims=True)
    return values * lax.rsqrt(mean_sq + epsilon)


def causal_conv(tail, inputs, taps):
    padded = jnp.concatenate([tail, inputs], axis=0).astype(jnp.float32)
    count = inputs.shape[0]
    total = jnp.zeros(inputs.shape, jnp.float32)
    for offset in range(CONV):
        total = total + taps[offset].astype(jnp.float32)[None, :] * padded[offset : offset + count]
    return jax.nn.silu(total)


def join_states(earlier, later):
    return (earlier[0] * later[0], later[0][:, None, None] * earlier[1] + later[1])


def shards(
    hidden,
    norm_gain,
    w_query,
    w_keyval,
    w_attn_out,
    w_inner,
    w_bc,
    w_dt,
    dt_bias,
    a_log,
    d_skip,
    conv_x,
    conv_bc,
    mamba_gain,
    w_mamba_out,
    cache,
    cache_len,
    tail_x,
    tail_bc,
    ssm_init,
):
    high = lax.Precision.HIGHEST
    own_rows = hidden[0]
    tokens = own_rows.shape[0]
    seq_pos = lax.axis_index("seq")
    mp_pos = lax.axis_index("mp")
    length = cache_len[0]
    whole = lax.all_gather(own_rows, "mp", axis=1, tiled=True)
    normed = (rms_scale(whole.astype(jnp.float32)) * norm_gain.astype(jnp.float32)).astype(
        jnp.bfloat16
    )
    positions = length + seq_pos * tokens + jnp.arange(tokens, dtype=jnp.int32)
    local_heads = w_query.shape[1] // HD
    query = rotate(
        jnp.dot(normed, w_query, preferred_element_type=jnp.float32).reshape(
            tokens, local_heads, HD
        ),
        positions,
    ).astype(jnp.bfloat16)
    projected = jnp.dot(normed, w_keyval, preferred_element_type=jnp.float32)
    roped = rotate(projected[:, None, :], positions)[:, 0, :]
    kv_block = jnp.where(mp_pos % 2 == 0, roped, projected).astype(jnp.bfloat16)
    bc_block = jnp.dot(normed, w_bc, preferred_element_type=jnp.float32).astype(jnp.bfloat16)
    bc_all = lax.all_gather(bc_block, "mp", axis=1, tiled=True)
    own_rows_kv = jnp.concatenate([cache[0], kv_block], axis=0)
    mp_size = lax.axis_size("mp")
    partner = lax.ppermute(own_rows_kv, "mp", [(i, i ^ 1) for i in range(mp_size)])
    is_key_block = mp_pos % 2 == 0
    group_rows = jnp.where(
        is_key_block,
        jnp.concatenate([own_rows_kv, partner], axis=1),
        jnp.concatenate([partner, own_rows_kv], axis=1),
    )
    inner = jnp.einsum("td,dkc->tkc", normed, w_inner, preferred_element_type=jnp.float32).astype(
        jnp.bfloat16
    )
    rim = CONV - 1
    prev_x, prev_bc = shifted((inner[tokens - rim :, 1], bc_all[tokens - rim :]), "seq", 1)
    first_block = seq_pos == 0
    prev_x = jnp.where(first_block, tail_x[0], prev_x)
    prev_bc = jnp.where(first_block, tail_bc[0], prev_bc)
    mamba_heads = dt_bias.shape[0]
    x_conv = causal_conv(prev_x, inner[:, 1], conv_x).reshape(tokens, mamba_heads, HD)
    bc_conv = causal_conv(prev_bc, bc_all, conv_bc)
    b_mat = bc_conv[:, :NS]
    c_mat = bc_conv[:, NS:]
    step_size = jax.nn.softplus(jnp.dot(normed, w_dt, preferred_element_type=jnp.float32) + dt_bias)
    log_decay = -step_size * jnp.exp(a_log)[None, :]
    cumulative = jnp.cumsum(log_decay, axis=0)
    pairs = jnp.dot(c_mat, b_mat.T, precision=high)
    gap = cumulative[:, None, :] - cumulative[None, :, :]
    token_ids = jnp.arange(tokens)
    lower = (token_ids[:, None] >= token_ids[None, :])[:, :, None]
    decay = jnp.where(lower, jnp.exp(jnp.where(lower, gap, 0.0)), 0.0)
    mixing = decay * pairs[:, :, None] * step_size[None, :, :]
    inner_out = jnp.einsum("tsh,shp->thp", mixing, x_conv, precision=high)
    to_end = jnp.exp(cumulative[-1][None, :] - cumulative) * step_size
    own_state = jnp.einsum("sh,shp,sn->hpn", to_end, x_conv, b_mat, precision=high)
    block_decay = jnp.exp(cumulative[-1])
    seq_size = lax.axis_size("seq")
    rows = HD // seq_size
    pieces = jnp.transpose(own_state.reshape(mamba_heads, seq_size, rows, NS), (1, 0, 2, 3))
    decays = jnp.broadcast_to(block_decay[None, :, None, None], (seq_size, mamba_heads, 1, NS))
    columns = lax.all_to_all(jnp.concatenate([pieces, decays], axis=2), "seq", 0, 0, tiled=True)
    carry = lax.dynamic_slice_in_dim(ssm_init[0], seq_pos * rows, rows, 1)
    entering = []
    for source in range(seq_size):
        entering.append(carry)
        part = columns[source]
        carry = part[:, rows:, :] * carry + part[:, :rows, :]
    entering = lax.all_to_all(jnp.stack(entering, axis=0), "seq", 0, 0, tiled=True)
    incoming = jnp.transpose(entering, (1, 0, 2, 3)).reshape(mamba_heads, HD, NS)
    carried = jnp.exp(cumulative)[:, :, None] * jnp.einsum(
        "tn,hpn->thp", c_mat, incoming, precision=high
    )
    mamba_y = inner_out + carried + d_skip[None, :, None] * x_conv
    state_after = block_decay[:, None, None] * incoming + own_state
    gated = mamba_y * jax.nn.silu(inner[:, 0].astype(jnp.float32).reshape(tokens, mamba_heads, HD))
    mixed = (
        rms_scale(gated).reshape(tokens, mamba_heads * HD) * mamba_gain.astype(jnp.float32)
    ).astype(jnp.bfloat16)
    cache_rows = cache.shape[1]
    shard_rows = cache_rows + tokens
    group = mp_pos * local_heads // (QH // KVH)
    query_index = seq_pos * tokens + jnp.arange(tokens, dtype=jnp.int32)
    scale = 1.0 / float(HD) ** 0.5
    piece = lax.all_gather(group_rows, "seq", axis=0, tiled=True)
    top = jnp.full((local_heads, tokens), negative, jnp.float32)
    count = piece.shape[0]
    index = jnp.arange(count, dtype=jnp.int32)
    owner = index // shard_rows
    offset = index % shard_rows
    in_cache = offset < cache_rows
    slot_ok = in_cache & (owner * cache_rows + offset < length)
    new_index = owner * tokens + offset - cache_rows
    valid = slot_ok[None, :] | (~in_cache)[None, :] & (new_index[None, :] <= query_index[:, None])
    scores = (
        jnp.einsum("qhd,kd->hqk", query, piece[:, :HD], preferred_element_type=jnp.float32) * scale
    )
    masked = jnp.where(valid[None], scores, negative)
    new_top = jnp.maximum(top, jnp.max(masked, axis=-1))
    weights = jnp.where(valid[None], jnp.exp(masked - new_top[:, :, None]), 0.0)
    total = jnp.sum(weights, axis=-1)
    accum = jnp.einsum(
        "hqk,kd->hqd",
        weights.astype(jnp.bfloat16),
        piece[:, HD : 2 * HD],
        preferred_element_type=jnp.float32,
    )
    top, total, accum = (new_top, total, accum)
    attended = jnp.transpose(accum / total[:, :, None], (1, 0, 2)).reshape(tokens, local_heads * HD)
    attended = attended.astype(jnp.bfloat16)
    term = jnp.dot(attended, w_attn_out, preferred_element_type=jnp.float32)
    term = term + jnp.dot(mixed, w_mamba_out, preferred_element_type=jnp.float32)
    summed = lax.psum_scatter(term, "mp", scatter_dimension=1, tiled=True)
    layer = (summed + own_rows.astype(jnp.float32)).astype(jnp.bfloat16)
    return (layer[None], kv_block[None], state_after[None, None])


def solution(mesh):
    placed = (
        P("req", "seq", "mp"),
        P(),
        P(None, "mp"),
        P(None, "mp"),
        P("mp", None),
        P(None, None, "mp"),
        P(None, "mp"),
        P(None, "mp"),
        P("mp"),
        P("mp"),
        P("mp"),
        P(None, "mp"),
        P(),
        P("mp"),
        P("mp", None),
        P("req", "seq", "mp"),
        P("req"),
        P("req", None, "mp"),
        P("req", None, None),
        P("req", "mp", None, None),
    )
    return jax.shard_map(
        shards,
        mesh=mesh,
        in_specs=placed,
        out_specs=(P("req", "seq", "mp"), P("req", "seq", "mp"), P("req", "seq", "mp", None, None)),
        check_vma=False,
    )
```

profile of v0, /device:TPU:1, one launch (start us, length us, event | category | flops | bytes accessed | tf_op | source)
XLA Modules:
  0.0 306.3 jit_solution(14901815859498077116)
XLA Ops:
  11.5 1.5 convert_reduce_fusion.3
  15.7 27.0 %all-gather.6.cloned.1.call-done = bf16[1,256,3072]{2,1,0:T(8,128)(2,1)} async-done(((bf16[1,256,768]{2,1,0:T(8,128)(2,1)}), bf16[1,256,3072]{2,1,0:T(8,128)(2,1)}) %all-gather.6.cloned.1.call-update) | async-done | bytes 1572880 | tf_op jit(solution)/shard_map/all_gather | solution.py:94
  42.7 1.9 fusion.9
  44.7 1.9 fusion.11
  52.8 2.2 convolution_convert_fusion
  55.0 2.1 fusion.98
  58.3 3.1 %collective-permute-start.1 = (bf16[3,384]{1,0:T(4,128)(2,1)S(1)}, bf16[3,384]{1,0:T(4,128)(2,1)S(1)}, u32[]{:S(2)}, u32[]{:S(2)}) collective-permute-start(bf16[3,384]{1,0:T(4,128)(2,1)S(1)} %copy-done.18), channel_id=1, source_target_pairs={{0,8},{8,16},{16,24},{24,32},{32,40},{40,48},{48,56},{56,64},{64,7... | collective-permute-start | bytes 6920 | tf_op jit(solution)/shard_map/ppermute | solution.py:19
  61.4 9.7 %all_gather.11 = bf16[256,512]{1,0:T(8,128)(2,1)S(1)} all-gather(bf16[256,128]{1,0:T(8,128)(2,1)S(1)} %convolution_convert_fusion), channel_id=1, replica_groups=mesh['seq'=32,'mp'=4,'req'=2] {'mp'}, dimensions={1}, use_global_device_ids=true | all-gather | bytes 327680 | tf_op jit(solution)/shard_map/all_gather | solution.py:110
  71.1 3.1 %collective-permute-start.2 = (bf16[3,512]{1,0:T(4,128)(2,1)S(1)}, bf16[3,512]{1,0:T(4,128)(2,1)S(1)}, u32[]{:S(2)}, u32[]{:S(2)}) collective-permute-start(bf16[3,512]{1,0:T(4,128)(2,1)S(1)} %slice.510), channel_id=1, source_target_pairs={{0,8},{8,16},{16,24},{24,32},{32,40},{40,48},{48,56},{56,64},{64,7... | collective-permute-start | bytes 9224 | tf_op jit(solution)/shard_map/ppermute | solution.py:19
  78.1 1.5 fusion.45
  80.9 9.3 %all-to-all-start = ((f32[32,3,5,256]{3,1,2,0:T(4,128)}), f32[32,3,5,256]{3,1,2,0:T(4,128)}, u32[]{:S(2)}, u32[]{:S(2)}) async-start(f32[32,3,5,256]{3,1,2,0:T(4,128)} %pad_maximum_fusion), calls=%async_computation | async-start | bytes 1310720 | tf_op jit(solution)/shard_map/all_to_all | solution.py:150
  90.3 1.8 maximum_select_fusion
  92.1 15.6 %and_or_fusion = pred[256,16384]{0,1:T(8,128)(4,1)} fusion(s32[256]{0:T(256)S(1)} %copy-done.22, s32[16384]{0:T(1024)S(1)} %copy-done.6, pred[16384]{0:T(1024)(128)(4,1)S(1)} %copy-done.7, pred[16384]{0:T(1024)(128)(4,1)S(1)} %get-tuple-element.103), kind=kLoop, calls=%fused_computation.7 | loop fusion | flops 12582912 | bytes 4293632 | tf_op jit(solution)/shard_map/or | solution.py:182
  109.1 1.9 multiply_cosine_fusion
  132.1 1.9 copy.77
  134.0 9.3 %all-to-all-start.1 = ((f32[32,3,4,256]{3,2,1,0:T(4,128)}), f32[32,3,4,256]{3,2,1,0:T(4,128)}, u32[]{:S(2)}, u32[]{:S(2)}) async-start(f32[32,3,4,256]{3,2,1,0:T(4,128)} %copy.77), calls=%async_computation.1 | async-start | bytes 786432 | tf_op jit(solution)/shard_map/all_to_all | solution.py:157
  143.5 2.6 fusion.99
  146.8 1.7 copy.86
  148.5 1.9 copy.79
  151.3 1.9 subtract_convert_fusion
  154.8 1.8 copy.78
  156.6 1.9 reshape.294
  158.5 1.5 convolution_multiply_fusion
  160.0 2.5 multiply_reduce_fusion
  162.7 40.1 %all-gather.4.cloned.1.call-done = bf16[16384,256]{0,1:T(8,128)(2,1)} async-done(((bf16[512,256]{0,1:T(8,128)(2,1)}), bf16[16384,256]{0,1:T(8,128)(2,1)}) %all-gather.4.cloned.1.call-update) | async-done | bytes 8388624 | tf_op jit(solution)/shard_map/all_gather | solution.py:173
  202.9 15.7 %fusion = (f32[2,256]{1,0:T(2,128)S(1)}, f32[16384,256,2]{1,0,2:T(8,128)}) fusion(pred[256,16384]{0,1:T(8,128)(4,1)} %and_or_fusion, bf16[256,2,64]{2,0,1:T(8,128)(2,1)} %get-tuple-element.50, bf16[256,2,64]{2,0,1:T(8,128)(2,1)} %get-tuple-element.49, bf16[16384,256]{0,1:T(8,128)(2,1)} %all-gather.4.cloned.1.call-done), kind=kOutput, calls=%fused_computation.2 | convolution fusion | flops 2172911104 | bytes 42207232 | tf_op jit(solution)/shard_map/qhd,kd->hqk/dot_general | solution.py:184
  218.5 15.7 %fusion.1 = f32[2,256]{1,0:T(2,128)S(1)} fusion(f32[16384,256,2]{1,0,2:T(8,128)} %get-tuple-element.98, f32[2,256]{1,0:T(2,128)S(1)} %broadcast_maximum_fusion, pred[256,16384]{0,1:T(8,128)(4,1)} %and_or_fusion), kind=kLoop, calls=%fused_computation.3 | loop fusion | flops 41942528 | bytes 37752832 | tf_op jit(solution)/shard_map/reduce_sum | solution.py:189
  234.2 17.2 %fusion.27 = bf16[256,2,128]{0,2,1:T(8,128)(2,1)S(1)} fusion(f32[16384,256,2]{1,0,2:T(8,128)} %get-tuple-element.98, f32[2,256]{1,0:T(2,128)S(1)} %broadcast_maximum_fusion, pred[256,16384]{0,1:T(8,128)(4,1)} %and_or_fusion, bf16[16384,256]{0,1:T(8,128)(2,1)} %all-gather.4.cloned.1.call-done, f32[256,2]{0,1:T(2,128)S(1)} %bitcast.367), kind=kOutput, calls=%fused_computation.30 | convolution fusion | flops 2189557760 | bytes 42078208 | tf_op jit(solution)/shard_map/hqk,kd->hqd/dot_general | solution.py:190
  251.4 2.0 fusion.100
  253.5 2.7 convolution_add_fusion
  257.8 40.0 %reduce-scatter.2.cloned.1.call-done = f32[256,768]{1,0:T(8,128)} async-done(((f32[256,3072]{1,0:T(8,128)}), f32[256,768]{1,0:T(8,128)}) %reduce-scatter.2.cloned.1.call-update) | async-done | bytes 786448 | tf_op jit(solution)/shard_map/reduce_scatter | solution.py:201
  297.8 2.0 fusion.40
  (166 shorter events, 46.3 us)
Async XLA Ops:
  7.2 246.3 %copy-start = (bf16[384,3072]{1,0:T(8,128)(2,1)S(1)}, bf16[384,3072]{1,0:T(8,128)(2,1)}, u32[]{:S(2)}) copy-start(bf16[384,3072]{1,0:T(8,128)(2,1)} %param.34) | copy-start | bytes 7077892
  7.2 35.5 %all-gather.6.cloned.1.call-start = ((), (), s32[]{:S(2)}) async-start(), calls=%async_computation.5 | async-start | bytes 1966080 | tf_op jit(solution)/shard_map/all_gather | solution.py:94
  10.9 46.6 %copy-start.4 = (bf16[1,256,128]{1,2,0:T(8,128)(2,1)}, bf16[1,256,128]{1,2,0:T(8,128)(2,1)S(1)}, u32[]{:S(2)}) copy-start(bf16[1,256,128]{1,2,0:T(8,128)(2,1)S(1)} %copy.66) | copy-start | bytes 196612
  10.9 46.2 %copy-start.21 = (f32[64]{0:T(128)}, f32[64]{0:T(128)S(1)}, u32[]{:S(2)}) copy-start(f32[64]{0:T(128)S(1)} %multiply_power_fusion) | copy-start | bytes 772
  11.5 45.6 %copy-start.16 = (f32[256]{0:T(256)}, f32[256]{0:T(256)S(1)}, u32[]{:S(2)}) copy-start(f32[256]{0:T(256)S(1)} %add_convert_fusion.1) | copy-start | bytes 3076
  42.7 3.9 %copy-start.25 = (bf16[3072,2,384]{2,1,0:T(2,128)(2,1)S(1)}, bf16[3072,2,384]{2,1,0:T(2,128)(2,1)}, u32[]{:S(2)}) copy-start(bf16[3072,2,384]{2,1,0:T(2,128)(2,1)} %param.25) | copy-start | bytes 14155780
  46.6 2.9 copy-start.1
  46.6 2.9 copy-start.8
  48.1 6.9 %copy-start.3 = (bf16[3072,128]{1,0:T(8,128)(2,1)S(1)}, bf16[3072,128]{1,0:T(8,128)(2,1)}, u32[]{:S(2)}) copy-start(bf16[3072,128]{1,0:T(8,128)(2,1)} %param.23) | copy-start | bytes 2359300
  51.3 7.1 %copy-start.18 = (bf16[3,384]{1,0:T(4,128)(2,1)S(1)}, bf16[3,384]{1,0:T(4,128)(2,1)}, u32[]{:S(2)}) copy-start(bf16[3,384]{1,0:T(4,128)(2,1)} %slice_bitcast_fusion.73) | copy-start | bytes 6916
  57.1 20.6 %copy-start.12 = (f32[1,512]{1,0:T(1,128)S(1)}, f32[1,512]{1,0:T(1,128)}, u32[]{:S(2)}) copy-start(f32[1,512]{1,0:T(1,128)} %get-tuple-element.90) | copy-start | bytes 6148
  57.1 20.6 %copy-start.13 = (f32[1,512]{1,0:T(1,128)S(1)}, f32[1,512]{1,0:T(1,128)}, u32[]{:S(2)}) copy-start(f32[1,512]{1,0:T(1,128)} %get-tuple-element.91) | copy-start | bytes 6148
  57.1 20.6 %copy-start.14 = (f32[1,512]{1,0:T(1,128)S(1)}, f32[1,512]{1,0:T(1,128)}, u32[]{:S(2)}) copy-start(f32[1,512]{1,0:T(1,128)} %get-tuple-element.92) | copy-start | bytes 6148
  57.1 20.6 %copy-start.15 = (f32[1,512]{1,0:T(1,128)S(1)}, f32[1,512]{1,0:T(1,128)}, u32[]{:S(2)}) copy-start(f32[1,512]{1,0:T(1,128)} %get-tuple-element.93) | copy-start | bytes 6148
  58.2 32.1 %collective-permute-start = (bf16[512,128]{0,1:T(8,128)(2,1)}, bf16[512,128]{0,1:T(8,128)(2,1)}, u32[]{:S(2)}, u32[]{:S(2)}) collective-permute-start(bf16[512,128]{0,1:T(8,128)(2,1)} %pad_maximum_fusion.1), channel_id=1, source_target_pairs={{0,2},{2,0},{4,6},{6,4},{1,3},{3,1},{5,7},{7,5},{8,10},{10,8},{12,... | collective-permute-start | bytes 393224 | tf_op jit(solution)/shard_map/ppermute | solution.py:113
  58.3 15.9 %collective-permute-start.1 = (bf16[3,384]{1,0:T(4,128)(2,1)S(1)}, bf16[3,384]{1,0:T(4,128)(2,1)S(1)}, u32[]{:S(2)}, u32[]{:S(2)}) collective-permute-start(bf16[3,384]{1,0:T(4,128)(2,1)S(1)} %copy-done.18), channel_id=1, source_target_pairs={{0,8},{8,16},{16,24},{24,32},{32,40},{40,48},{48,56},{56,64},{64,7... | collective-permute-start | bytes 6920 | tf_op jit(solution)/shard_map/ppermute | solution.py:19
  71.1 5.7 %collective-permute-start.2 = (bf16[3,512]{1,0:T(4,128)(2,1)S(1)}, bf16[3,512]{1,0:T(4,128)(2,1)S(1)}, u32[]{:S(2)}, u32[]{:S(2)}) collective-permute-start(bf16[3,512]{1,0:T(4,128)(2,1)S(1)} %slice.510), channel_id=1, source_target_pairs={{0,8},{8,16},{16,24},{24,32},{32,40},{40,48},{48,56},{56,64},{64,7... | collective-permute-start | bytes 9224 | tf_op jit(solution)/shard_map/ppermute | solution.py:19
  75.0 4.9 %copy-start.19 = (f32[3]{0:T(128)S(1)}, f32[3]{0:T(128)}, u32[]{:S(2)}) copy-start(f32[3]{0:T(128)} %exp.54) | copy-start | bytes 40
  76.8 13.4 %copy-start.5 = (bf16[1,256,128]{1,2,0:T(8,128)(2,1)S(1)}, bf16[1,256,128]{1,2,0:T(8,128)(2,1)}, u32[]{:S(2)}) copy-start(bf16[1,256,128]{1,2,0:T(8,128)(2,1)} %copy-done.4) | copy-start | bytes 196612
  77.6 14.4 %copy-start.6 = (s32[16384]{0:T(1024)S(1)}, s32[16384]{0:T(1024)}, u32[]{:S(2)}) copy-start(s32[16384]{0:T(1024)} %fusion.80) | copy-start | bytes 196612
  77.7 14.4 %copy-start.7 = (pred[16384]{0:T(1024)(128)(4,1)S(1)}, pred[16384]{0:T(1024)(128)(4,1)}, u32[]{:S(2)}) copy-start(pred[16384]{0:T(1024)(128)(4,1)} %get-tuple-element.104) | copy-start | bytes 49156
  77.7 14.4 %copy-start.22 = (s32[256]{0:T(256)S(1)}, s32[256]{0:T(256)}, u32[]{:S(2)}) copy-start(s32[256]{0:T(256)} %iota_add_fusion) | copy-start | bytes 3076
  79.5 28.2 %copy-start.23 = (bf16[384]{0:T(512)(128)(2,1)S(1)}, bf16[384]{0:T(512)(128)(2,1)}, u32[]{:S(2)}) copy-start(bf16[384]{0:T(512)(128)(2,1)} %param.33) | copy-start | bytes 2308
  80.9 30.1 %all-to-all-start = ((f32[32,3,5,256]{3,1,2,0:T(4,128)}), f32[32,3,5,256]{3,1,2,0:T(4,128)}, u32[]{:S(2)}, u32[]{:S(2)}) async-start(f32[32,3,5,256]{3,1,2,0:T(4,128)} %pad_maximum_fusion), calls=%async_computation | async-start | bytes 1310720 | tf_op jit(solution)/shard_map/all_to_all | solution.py:150
  90.2 112.7 %all-gather.4.cloned.1.call-start = ((), (), s32[]{:S(2)}) async-start(), calls=%async_computation.3 | async-start | bytes 8650752 | tf_op jit(solution)/shard_map/all_gather | solution.py:173
  134.0 20.8 %all-to-all-start.1 = ((f32[32,3,4,256]{3,2,1,0:T(4,128)}), f32[32,3,4,256]{3,2,1,0:T(4,128)}, u32[]{:S(2)}, u32[]{:S(2)}) async-start(f32[32,3,4,256]{3,2,1,0:T(4,128)} %copy.77), calls=%async_computation.1 | async-start | bytes 786432 | tf_op jit(solution)/shard_map/all_to_all | solution.py:157
  143.3 15.2 %copy-start.9 = (f32[256,3]{0,1:T(4,128)S(1)}, f32[256,3]{0,1:T(4,128)}, u32[]{:S(2)}) copy-start(f32[256,3]{0,1:T(4,128)} %get-tuple-element.94) | copy-start | bytes 9220
  143.3 16.7 %copy-start.11 = (f32[1,3,2,128]{3,1,2,0:T(4,128)S(1)}, f32[1,3,2,128]{3,1,2,0:T(4,128)}, u32[]{:S(2)}) copy-start(f32[1,3,2,128]{3,1,2,0:T(4,128)} %copy-done.10) | copy-start | bytes 9220
  143.3 16.7 %copy-start.17 = (f32[256,3]{0,1:T(4,128)S(1)}, f32[256,3]{0,1:T(4,128)}, u32[]{:S(2)}) copy-start(f32[256,3]{0,1:T(4,128)} %get-tuple-element.88) | copy-start | bytes 9220
  143.3 154.5 %reduce-scatter.2.cloned.1.call-start = ((), (), s32[]{:S(2)}) async-start(), calls=%async_computation.4 | async-start | bytes 3932160 | tf_op jit(solution)/shard_map/reduce_scatter | solution.py:201
  253.4 3.5 %copy-start.2 = (f32[3,128,256]{2,1,0:T(8,128)S(1)}, f32[3,128,256]{2,1,0:T(8,128)}, u32[]{:S(2)}) copy-start(f32[3,128,256]{2,1,0:T(8,128)} %reshape.294) | copy-start | bytes 1179652
  253.5 3.5 %copy-start.20 = (f32[3]{0:T(128)S(1)}, f32[3]{0:T(128)}, u32[]{:S(2)}) copy-start(f32[3]{0:T(128)} %exp.54) | copy-start | bytes 40
  (2 other events, 3.6 us)
Sparse Core Ops, SparseCore 0:
  9.8 32.8 all-gather.5
  93.5 109.3 all-gather.3
  256.3 41.4 reduce-scatter.1
where the time goes:
time: 308 us; the launch traced here: 306 us
  waiting for transfers between devices  108 us (35%)
  other arithmetic  75.5 us (25%)
  matrix products  53 us (17%)
  starting transfers between devices  25.2 us (8%)
  local copies, waits for them, and re-layouts  19.5 us (6%)
  between operations  15.1 us (5%)
  blocking collectives  9.69 us (3%)
    all_gather x1, waiting for transfers between devices, shards(): piece = lax.all_gather(group_rows, 'seq', axis=0, tiled=True)  40.1 us
    reduce_scatter x1, waiting for transfers between devices, shards(): summed = lax.psum_scatter(term, 'mp', scatter_dimension=1, tiled=True)  40 us
    all_gather x1, waiting for transfers between devices, shards(): whole = lax.all_gather(own_rows, 'mp', axis=1, tiled=True)  27 us
    unnamed x31, other arithmetic  18.3 us
    dot_general x1, matrix products, shards(): jnp.einsum('hqk,kd->hqd', weights.astype(jnp.bfloat16), piece[:, HD:2 * H...  17.2 us
    reduce_sum x1, other arithmetic, shards(): total = jnp.sum(weights, axis=-1)  15.7 us
    dot_general x1, matrix products, shards(): jnp.einsum('qhd,kd->hqk', query, piece[:, :HD], preferred_element_type=jn...  15.7 us
    or x1, other arithmetic, shards(): slot_ok[None, :]  15.6 us
  transfers between devices with their start and end apart: 8, of which 4 were waited for; matrix products, arithmetic and copies ran while one was open for 25% of the time, Pallas kernels for 0%

commit v1 on v0

--- a/solution.py
+++ b/solution.py
@@ -91,7 +91,9 @@
     seq_pos = lax.axis_index("seq")
     mp_pos = lax.axis_index("mp")
     length = cache_len[0]
-    whole = lax.all_gather(own_rows, "mp", axis=1, tiled=True)
+    whole = jnp.concatenate(
+        lax.all_to_all(jnp.stack([own_rows] * lax.axis_size("mp")), "mp", 0, 0), axis=1
+    )
     normed = (rms_scale(whole.astype(jnp.float32)) * norm_gain.astype(jnp.float32)).astype(
         jnp.bfloat16
     )

time: 308 us -> 283 us (0.919)
  waiting for transfers between devices: 108 us -> 75.9 us
  starting transfers between devices: 25.2 us -> 33.1 us
  other arithmetic: 75.5 us -> 69.3 us
  local copies, waits for them, and re-layouts: 19.5 us -> 23.2 us
    all_gather x1 -> x0, waiting for transfers between devices: 27 us -> none  [shards(): whole = lax.all_gather(own_rows, 'mp', axis=1, tiled=True)]
    all_gather x1, waiting for transfers between devices: 40.1 us -> 15.1 us  [shards(): piece = lax.all_gather(group_rows, 'seq', axis=0, tiled=True)]
    all_to_all x1, waiting for transfers between devices: 0.49 us -> 11.8 us  [shards(): lax.all_to_all(jnp.stack(entering, axis=0), 'seq', 0, 0, tiled=True)]
    all_to_all x1, waiting for transfers between devices: 0.01 us -> 9.16 us  [shards(): lax.all_to_all(jnp.concatenate([pieces, decays], axis=2), 'seq', 0, 0, ti...]
    all_to_all x0 -> x1, starting transfers between devices: none -> 4.99 us  [shards(): lax.all_to_all(jnp.stack([own_rows] * lax.axis_size('mp')), 'mp', 0, 0)]
  transfers between devices with their start and end apart: 8 -> 8, of which waited for: 4 -> 4; matrix products, arithmetic and copies ran while one was open for 25% -> 26% of each run, Pallas kernels for 0% -> 0%
where the time goes in v1:
time: 283 us; the launch traced here: 282 us
  waiting for transfers between devices  75.9 us (27%)
  other arithmetic  69.3 us (24%)
  matrix products  55.5 us (20%)
  starting transfers between devices  33.1 us (12%)
  local copies, waits for them, and re-layouts  23.2 us (8%)
  between operations  15.3 us (5%)
  blocking collectives  9.65 us (3%)
    reduce_scatter x1, waiting for transfers between devices, shards(): summed = lax.psum_scatter(term, 'mp', scatter_dimension=1, tiled=True)  39.9 us
    unnamed x31, other arithmetic  18.3 us
    dot_general x1, matrix products, shards(): jnp.einsum('hqk,kd->hqd', weights.astype(jnp.bfloat16), piece[:, HD:2 * H...  17.2 us
    reduce_sum x1, other arithmetic, shards(): total = jnp.sum(weights, axis=-1)  15.7 us
    or x1, other arithmetic, shards(): slot_ok[None, :]  15.6 us
    dot_general x1, matrix products, shards(): jnp.einsum('qhd,kd->hqk', query, piece[:, :HD], preferred_element_type=jn...  15.6 us
    all_gather x1, waiting for transfers between devices, shards(): piece = lax.all_gather(group_rows, 'seq', axis=0, tiled=True)  15.1 us
    all_to_all x1, starting transfers between devices, shards(): lax.all_to_all(jnp.concatenate([pieces, decays], axis=2), 'seq', 0, 0, ti...  11.9 us
  transfers between devices with their start and end apart: 8, of which 4 were waited for; matrix products, arithmetic and copies ran while one was open for 26% of the time, Pallas kernels for 0%

profile of v1, /device:TPU:1, one launch (start us, length us, event | category | flops | bytes accessed | tf_op | source)
XLA Modules:
  0.0 282.0 jit_solution(8555985153625332375)
XLA Ops:
  7.2 2.4 stack.100
  9.6 5.0 %all-to-all-start = ((bf16[4,256,768]{2,1,0:T(8,128)(2,1)}), bf16[4,256,768]{2,1,0:T(8,128)(2,1)}, u32[]{:S(2)}, u32[]{:S(2)}) async-start(bf16[4,256,768]{2,1,0:T(8,128)(2,1)} %stack.100), calls=%async_computation | async-start | bytes 3145728 | tf_op jit(solution)/shard_map/all_to_all | solution.py:95
  15.4 15.6 %and_or_fusion = pred[256,16384]{0,1:T(8,128)(4,1)} fusion(s32[256]{0:T(256)S(1)} %iota_add_fusion, s32[16384]{0:T(1024)S(1)} %fusion.78, pred[16384]{0:T(1024)(128)(4,1)S(1)} %get-tuple-element.105, pred[16384]{0:T(1024)(128)(4,1)S(1)} %get-tuple-element.104), kind=kLoop, calls=%fused_computation.7 | loop fusion | flops 12582912 | bytes 4293632 | tf_op jit(solution)/shard_map/or | solution.py:184
  32.3 2.6 copy.108
  35.1 2.6 copy.84
  37.6 1.8 multiply_reduce_fusion
  39.5 1.9 fusion.10
  44.2 2.1 fusion.95
  46.2 4.3 %fusion.12 = bf16[256,2,384]{2,0,1:T(8,128)(2,1)S(1)} fusion(bf16[3072,2,384]{2,1,0:T(2,128)(2,1)} %param.25, bf16[256,3072]{0,1:T(8,128)(2,1)} %copy-done.1), kind=kOutput, calls=%fused_computation.20 | convolution fusion | flops 1208156160 | bytes 6684672 | tf_op jit(solution)/shard_map/td,dkc->tkc/dot_general | solution.py:122
  53.0 3.3 %collective-permute-start.1 = (bf16[3,384]{1,0:T(4,128)(2,1)S(1)}, bf16[3,384]{1,0:T(4,128)(2,1)S(1)}, u32[]{:S(2)}, u32[]{:S(2)}) collective-permute-start(bf16[3,384]{1,0:T(4,128)(2,1)S(1)} %slice_bitcast_fusion.73), channel_id=1, source_target_pairs={{0,8},{8,16},{16,24},{24,32},{32,40},{40,48},{48,56},{56,64},{64,7... | collective-permute-start | bytes 6920 | tf_op jit(solution)/shard_map/ppermute | solution.py:19
  57.9 1.8 slice_convert_fusion
  59.8 2.0 convolution_convert_fusion
  61.8 9.7 %all_gather.7 = bf16[256,512]{1,0:T(8,128)(2,1)S(1)} all-gather(bf16[256,128]{1,0:T(8,128)(2,1)S(1)} %convolution_convert_fusion), channel_id=1, replica_groups=mesh['seq'=32,'mp'=4,'req'=2] {'mp'}, dimensions={1}, use_global_device_ids=true | all-gather | bytes 327680 | tf_op jit(solution)/shard_map/all_gather | solution.py:112
  71.4 3.2 %collective-permute-start.2 = (bf16[3,512]{1,0:T(4,128)(2,1)S(1)}, bf16[3,512]{1,0:T(4,128)(2,1)S(1)}, u32[]{:S(2)}, u32[]{:S(2)}) collective-permute-start(bf16[3,512]{1,0:T(4,128)(2,1)S(1)} %slice.510), channel_id=1, source_target_pairs={{0,8},{8,16},{16,24},{24,32},{32,40},{40,48},{48,56},{56,64},{64,7... | collective-permute-start | bytes 9224 | tf_op jit(solution)/shard_map/ppermute | solution.py:19
  79.2 11.9 %all-to-all-start.1 = ((f32[32,3,5,256]{3,1,2,0:T(4,128)}), f32[32,3,5,256]{3,1,2,0:T(4,128)}, u32[]{:S(2)}, u32[]{:S(2)}) async-start(f32[32,3,5,256]{3,1,2,0:T(4,128)} %pad_maximum_fusion), calls=%async_computation.1 | async-start | bytes 1310720 | tf_op jit(solution)/shard_map/all_to_all | solution.py:152
  93.5 1.9 copy.99
  95.4 3.1 %multiply_convert_fusion = bf16[4,256,768]{1,2,0:T(8,128)(2,1)} fusion(bf16[4,256,768]{1,2,0:T(8,128)(2,1)} %copy.84, f32[4,768]{1,0:T(4,128)} %mul.664, f32[256]{0:T(256)} %copy-done.9), kind=kLoop, calls=%fused_computation.17 | loop fusion | flops 3145728 | bytes 3159040 | tf_op jit(solution)/shard_map/convert.13
  98.5 9.2 %all-to-all-done.1 = f32[32,3,5,256]{3,1,2,0:T(4,128)} async-done(((f32[32,3,5,256]{3,1,2,0:T(4,128)}), f32[32,3,5,256]{3,1,2,0:T(4,128)}, u32[]{:S(2)}, u32[]{:S(2)}) %all-to-all-start.1) | async-done | bytes 491552 | tf_op jit(solution)/shard_map/all_to_all | solution.py:152
  128.7 1.9 copy.97
  130.6 7.8 %all-to-all-start.2 = ((f32[32,3,4,256]{3,2,1,0:T(4,128)}), f32[32,3,4,256]{3,2,1,0:T(4,128)}, u32[]{:S(2)}, u32[]{:S(2)}) async-start(f32[32,3,4,256]{3,2,1,0:T(4,128)} %copy.97), calls=%async_computation.2 | async-start | bytes 786432 | tf_op jit(solution)/shard_map/all_to_all | solution.py:159
  138.6 2.6 fusion.96
  143.0 11.8 %all-to-all-done.2 = f32[32,3,4,256]{3,2,1,0:T(4,128)} async-done(((f32[32,3,4,256]{3,2,1,0:T(4,128)}), f32[32,3,4,256]{3,2,1,0:T(4,128)}, u32[]{:S(2)}, u32[]{:S(2)}) %all-to-all-start.2) | async-done | bytes 393248 | tf_op jit(solution)/shard_map/all_to_all | solution.py:159
  156.5 1.9 reshape.307
  159.9 2.6 multiply_reduce_fusion.1
  163.3 15.1 %all-gather.2.cloned.1.call-done = bf16[16384,256]{0,1:T(8,128)(2,1)} async-done(((bf16[512,256]{0,1:T(8,128)(2,1)}), bf16[16384,256]{0,1:T(8,128)(2,1)}) %all-gather.2.cloned.1.call-update) | async-done | bytes 8388624 | tf_op jit(solution)/shard_map/all_gather | solution.py:175
  178.4 15.6 %fusion = (f32[2,256]{1,0:T(2,128)S(1)}, f32[16384,256,2]{1,0,2:T(8,128)}) fusion(pred[256,16384]{0,1:T(8,128)(4,1)} %and_or_fusion, bf16[256,2,64]{0,2,1:T(8,128)(2,1)} %get-tuple-element.86, bf16[256,2,64]{0,2,1:T(8,128)(2,1)} %get-tuple-element.85, bf16[16384,256]{0,1:T(8,128)(2,1)} %all-gather.2.cloned.1.call-done), kind=kOutput, calls=%fused_computation.2 | convolution fusion | flops 2172911104 | bytes 42076160 | tf_op jit(solution)/shard_map/qhd,kd->hqk/dot_general | solution.py:186
  194.0 15.7 %fusion.1 = f32[2,256]{1,0:T(2,128)S(1)} fusion(f32[16384,256,2]{1,0,2:T(8,128)} %get-tuple-element.99, f32[2,256]{1,0:T(2,128)S(1)} %broadcast_maximum_fusion, pred[256,16384]{0,1:T(8,128)(4,1)} %and_or_fusion), kind=kLoop, calls=%fused_computation.3 | loop fusion | flops 41942528 | bytes 37752832 | tf_op jit(solution)/shard_map/reduce_sum | solution.py:191
  209.7 17.2 %fusion.26 = bf16[256,2,128]{0,2,1:T(8,128)(2,1)S(1)} fusion(f32[16384,256,2]{1,0,2:T(8,128)} %get-tuple-element.99, f32[2,256]{1,0:T(2,128)S(1)} %broadcast_maximum_fusion, pred[256,16384]{0,1:T(8,128)(4,1)} %and_or_fusion, bf16[16384,256]{0,1:T(8,128)(2,1)} %all-gather.2.cloned.1.call-done, f32[256,2]{0,1:T(2,128)S(1)} %bitcast.379), kind=kOutput, calls=%fused_computation.30 | convolution fusion | flops 2189557760 | bytes 42078208 | tf_op jit(solution)/shard_map/hqk,kd->hqd/dot_general | solution.py:192
  226.9 2.0 fusion.97
  228.9 2.7 convolution_add_fusion
  233.3 39.9 %reduce-scatter.2.cloned.1.call-done = f32[256,768]{1,0:T(8,128)} async-done(((f32[256,3072]{1,0:T(8,128)}), f32[256,768]{1,0:T(8,128)}) %reduce-scatter.2.cloned.1.call-update) | async-done | bytes 786448 | tf_op jit(solution)/shard_map/reduce_scatter | solution.py:203
  273.1 2.0 fusion.38
  (161 shorter events, 43.7 us)
Async XLA Ops:
  7.2 221.7 %copy-start = (bf16[384,3072]{1,0:T(8,128)(2,1)S(1)}, bf16[384,3072]{1,0:T(8,128)(2,1)}, u32[]{:S(2)}) copy-start(bf16[384,3072]{1,0:T(8,128)(2,1)} %param.34) | copy-start | bytes 7077892
  9.6 21.4 %copy-start.6 = (bf16[3072]{0:T(1024)(128)(2,1)S(1)}, bf16[3072]{0:T(1024)(128)(2,1)}, u32[]{:S(2)}) copy-start(bf16[3072]{0:T(1024)(128)(2,1)} %param.21) | copy-start | bytes 18436
  9.6 22.0 %copy-start.21 = (f32[3]{0:T(128)S(1)}, f32[3]{0:T(128)}, u32[]{:S(2)}) copy-start(f32[3]{0:T(128)} %param.29) | copy-start | bytes 40
  9.6 22.0 %copy-start.19 = (bf16[384]{0:T(512)(128)(2,1)S(1)}, bf16[384]{0:T(512)(128)(2,1)}, u32[]{:S(2)}) copy-start(bf16[384]{0:T(512)(128)(2,1)} %param.33) | copy-start | bytes 2308
  9.6 22.6 %copy-start.5 = (bf16[1,256,128]{2,1,0:T(8,128)(2,1)S(1)}, bf16[1,256,128]{2,1,0:T(8,128)(2,1)}, u32[]{:S(2)}) copy-start(bf16[1,256,128]{2,1,0:T(8,128)(2,1)} %param.35) | copy-start | bytes 196612
  9.6 25.4 %all-to-all-start = ((bf16[4,256,768]{2,1,0:T(8,128)(2,1)}), bf16[4,256,768]{2,1,0:T(8,128)(2,1)}, u32[]{:S(2)}, u32[]{:S(2)}) async-start(bf16[4,256,768]{2,1,0:T(8,128)(2,1)} %stack.100), calls=%async_computation | async-start | bytes 3145728 | tf_op jit(solution)/shard_map/all_to_all | solution.py:95
  14.6 20.4 %copy-start.8 = (bf16[4,384]{1,0:T(4,128)(2,1)S(1)}, bf16[4,384]{1,0:T(4,128)(2,1)}, u32[]{:S(2)}) copy-start(bf16[4,384]{1,0:T(4,128)(2,1)} %param.31) | copy-start | bytes 9220
  14.6 20.4 %copy-start.7 = (bf16[4,512]{1,0:T(4,128)(2,1)S(1)}, bf16[4,512]{1,0:T(4,128)(2,1)}, u32[]{:S(2)}) copy-start(bf16[4,512]{1,0:T(4,128)(2,1)} %param.32) | copy-start | bytes 12292
  14.6 163.8 %all-gather.2.cloned.1.call-start = ((), (), s32[]{:S(2)}) async-start(), calls=%async_computation.4 | async-start | bytes 8650752 | tf_op jit(solution)/shard_map/all_gather | solution.py:175
  34.9 7.6 %copy-start.20 = (bf16[3072,3]{0,1:T(4,128)(2,1)S(1)}, bf16[3072,3]{0,1:T(4,128)(2,1)}, u32[]{:S(2)}) copy-start(bf16[3072,3]{0,1:T(4,128)(2,1)} %param.27) | copy-start | bytes 55300
  34.9 7.6 %copy-start.22 = (f32[3]{0:T(128)S(1)}, f32[3]{0:T(128)}, u32[]{:S(2)}) copy-start(f32[3]{0:T(128)} %param.28) | copy-start | bytes 40
  34.9 15.6 %copy-start.18 = (f32[64]{0:T(128)}, f32[64]{0:T(128)S(1)}, u32[]{:S(2)}) copy-start(f32[64]{0:T(128)S(1)} %multiply_power_fusion) | copy-start | bytes 772
  35.0 15.6 %copy-start.12 = (f32[256]{0:T(256)}, f32[256]{0:T(256)S(1)}, u32[]{:S(2)}) copy-start(f32[256]{0:T(256)S(1)} %add_convert_fusion.2) | copy-start | bytes 3076
  39.5 4.7 %copy-start.9 = (f32[256]{0:T(256)}, f32[256]{0:T(256)S(1)}, u32[]{:S(2)}) copy-start(f32[256]{0:T(256)S(1)} %add_rsqrt_fusion.1) | copy-start | bytes 3076
  41.4 1.2 copy-start.1
  46.2 13.5 %copy-start.3 = (bf16[3072,128]{1,0:T(8,128)(2,1)S(1)}, bf16[3072,128]{1,0:T(8,128)(2,1)}, u32[]{:S(2)}) copy-start(bf16[3072,128]{1,0:T(8,128)(2,1)} %param.26) | copy-start | bytes 2359300
  50.5 0.7 copy-start.4
  50.6 24.1 %copy-start.15 = (bf16[1,3,384]{2,1,0:T(4,128)(2,1)S(1)}, bf16[1,3,384]{2,1,0:T(4,128)(2,1)}, u32[]{:S(2)}) copy-start(bf16[1,3,384]{2,1,0:T(4,128)(2,1)} %param.37) | copy-start | bytes 6916
  50.9 25.0 %copy-start.13 = (bf16[1,3,512]{2,1,0:T(4,128)(2,1)S(1)}, bf16[1,3,512]{2,1,0:T(4,128)(2,1)}, u32[]{:S(2)}) copy-start(bf16[1,3,512]{2,1,0:T(4,128)(2,1)} %param.38) | copy-start | bytes 9220
  51.3 5.3 %collective-permute-start = (bf16[512,128]{0,1:T(8,128)(2,1)S(1)}, bf16[512,128]{0,1:T(8,128)(2,1)S(1)}, u32[]{:S(2)}, u32[]{:S(2)}) collective-permute-start(bf16[512,128]{0,1:T(8,128)(2,1)S(1)} %pad_maximum_fusion.1), channel_id=1, source_target_pairs={{0,2},{2,0},{4,6},{6,4},{1,3},{3,1},{5,7},{7,5},{8,10},{10,8},{12,... | collective-permute-start | bytes 393224 | tf_op jit(solution)/shard_map/ppermute | solution.py:115
  53.0 23.0 %copy-start.10 = (f32[1,3,2,128]{3,1,2,0:T(4,128)}, f32[1,3,2,128]{3,1,2,0:T(4,128)S(1)}, u32[]{:S(2)}) copy-start(f32[1,3,2,128]{3,1,2,0:T(4,128)S(1)} %copy.133) | copy-start | bytes 9220
  53.0 21.7 %collective-permute-start.1 = (bf16[3,384]{1,0:T(4,128)(2,1)S(1)}, bf16[3,384]{1,0:T(4,128)(2,1)S(1)}, u32[]{:S(2)}, u32[]{:S(2)}) collective-permute-start(bf16[3,384]{1,0:T(4,128)(2,1)S(1)} %slice_bitcast_fusion.73), channel_id=1, source_target_pairs={{0,8},{8,16},{16,24},{24,32},{32,40},{40,48},{48,56},{56,64},{64,7... | collective-permute-start | bytes 6920 | tf_op jit(solution)/shard_map/ppermute | solution.py:19
  71.4 6.7 %copy-start.16 = (f32[3]{0:T(128)}, f32[3]{0:T(128)S(1)}, u32[]{:S(2)}) copy-start(f32[3]{0:T(128)S(1)} %exp.54) | copy-start | bytes 40
  71.4 4.5 %collective-permute-start.2 = (bf16[3,512]{1,0:T(4,128)(2,1)S(1)}, bf16[3,512]{1,0:T(4,128)(2,1)S(1)}, u32[]{:S(2)}, u32[]{:S(2)}) collective-permute-start(bf16[3,512]{1,0:T(4,128)(2,1)S(1)} %slice.510), channel_id=1, source_target_pairs={{0,8},{8,16},{16,24},{24,32},{32,40},{40,48},{48,56},{56,64},{64,7... | collective-permute-start | bytes 9224 | tf_op jit(solution)/shard_map/ppermute | solution.py:19
  79.2 28.4 %all-to-all-start.1 = ((f32[32,3,5,256]{3,1,2,0:T(4,128)}), f32[32,3,5,256]{3,1,2,0:T(4,128)}, u32[]{:S(2)}, u32[]{:S(2)}) async-start(f32[32,3,5,256]{3,1,2,0:T(4,128)} %pad_maximum_fusion), calls=%async_computation.1 | async-start | bytes 1310720 | tf_op jit(solution)/shard_map/all_to_all | solution.py:152
  130.5 29.3 %copy-start.11 = (f32[1,3,2,128]{3,1,2,0:T(4,128)S(1)}, f32[1,3,2,128]{3,1,2,0:T(4,128)}, u32[]{:S(2)}) copy-start(f32[1,3,2,128]{3,1,2,0:T(4,128)} %copy-done.10) | copy-start | bytes 9220
  130.5 29.4 %copy-start.14 = (f32[256,3]{0,1:T(4,128)S(1)}, f32[256,3]{0,1:T(4,128)}, u32[]{:S(2)}) copy-start(f32[256,3]{0,1:T(4,128)} %get-tuple-element.89) | copy-start | bytes 9220
  130.6 24.2 %all-to-all-start.2 = ((f32[32,3,4,256]{3,2,1,0:T(4,128)}), f32[32,3,4,256]{3,2,1,0:T(4,128)}, u32[]{:S(2)}, u32[]{:S(2)}) async-start(f32[32,3,4,256]{3,2,1,0:T(4,128)} %copy.97), calls=%async_computation.2 | async-start | bytes 786432 | tf_op jit(solution)/shard_map/all_to_all | solution.py:159
  138.3 134.8 %reduce-scatter.2.cloned.1.call-start = ((), (), s32[]{:S(2)}) async-start(), calls=%async_computation.5 | async-start | bytes 3932160 | tf_op jit(solution)/shard_map/reduce_scatter | solution.py:203
  228.9 3.5 %copy-start.2 = (f32[3,128,256]{2,1,0:T(8,128)S(1)}, f32[3,128,256]{2,1,0:T(8,128)}, u32[]{:S(2)}) copy-start(f32[3,128,256]{2,1,0:T(8,128)} %reshape.307) | copy-start | bytes 1179652
  228.9 3.5 %copy-start.17 = (f32[3]{0:T(128)S(1)}, f32[3]{0:T(128)}, u32[]{:S(2)}) copy-start(f32[3]{0:T(128)} %copy-done.16) | copy-start | bytes 40
Sparse Core Ops, SparseCore 0:
  57.5 120.8 all-gather.1
  231.8 41.3 reduce-scatter.1
